TPU v7x, 256 devices: a whole 4x4x8 slice. The times are simulated.
256 devices in a mesh: dp: 8 (over x, core), expert: 32 (over z, y).
Axes of the slice: x: 4, y: 4, z: 8, core: 2. Of those that a mesh axis runs over, the one named last changes fastest.
Arguments:
- tokens: bfloat16 [8192, 7168], P('expert', 'dp'), may hold values from -6 to 6
- grad_out: bfloat16 [8192, 7168], P('expert', 'dp'), may hold values from -6 to 6
- route_ids: int32 [8192, 8], P('expert'), may hold values from 0 to 255, all different within a row; in each aligned block of 256 rows (0 to 255, 256 to 511, ...) at most 12 rows name the same one
- route_gates: float32 [8192, 8], P('expert'), may hold values from 0.1 to 1
- w_gate: bfloat16 [32, 7168, 1024], P('expert', 'dp'), may hold values from -0.0625 to 0.0625
- w_up: bfloat16 [32, 7168, 1024], P('expert', 'dp'), may hold values from -0.0625 to 0.0625
- w_down: bfloat16 [32, 1024, 7168], P('expert', None, 'dp'), may hold values from -0.1875 to 0.1875
- shared_gate: bfloat16 [7168, 1024], P('dp', 'expert'), may hold values from -0.0625 to 0.0625
- shared_up: bfloat16 [7168, 1024], P('dp', 'expert'), may hold values from -0.0625 to 0.0625
- shared_down: bfloat16 [1024, 7168], P('expert', 'dp'), may hold values from -0.1875 to 0.1875
Outputs:
- grad_tokens: bfloat16 [8192, 7168], P('expert', 'dp')
- grad_gate: bfloat16 [32, 7168, 1024], P('expert', 'dp')
- grad_up: bfloat16 [32, 7168, 1024], P('expert', 'dp')
- grad_down: bfloat16 [32, 1024, 7168], P('expert', None, 'dp')
- grad_shared_gate: float32 [7168, 1024], P('dp', 'expert')
- grad_shared_up: float32 [7168, 1024], P('dp', 'expert')
- grad_shared_down: float32 [1024, 7168], P('expert', 'dp')
Inputs may be any that keep to these rules, and one draw needn't show every extreme that they name: `route_ids`: each row names 8 different experts; in each aligned block of 256 rows no expert is named by more than 12 rows, a bound that some block reaches.
All inputs are finite; a program needn't handle non-finite values.
Results may differ from a plain program's by a relative error of at most 0.018.
Values may be sent and summed in bfloat16 or wider, within the bound.
No kernel may reach another device: no remote copies, remote signals or barrier semaphores. Data moves between devices by JAX's collectives and lax.ppermute only.
A program may use at most 128 MiB of HBM per device.

v0:
```python
import jax
import jax.numpy as jnp
from jax import lax
from jax.sharding import PartitionSpec as P

CAP = 12


def silu_parts(pre):
    sigmoid_val = jax.nn.sigmoid(pre)
    return (pre * sigmoid_val, sigmoid_val * (1.0 + pre * (1.0 - sigmoid_val)))


def contract_rows(left, right):
    return lax.dot_general(
        left, right, (((0,), (0,)), ((), ())), preferred_element_type=jnp.float32
    )


def contract_cols(left, right):
    return lax.dot_general(
        left, right, (((1,), (1,)), ((), ())), preferred_element_type=jnp.float32
    )


def hidden_products(part_gate, part_up, part_act):
    silu_val, silu_slope = silu_parts(part_gate)
    activated = (silu_val * part_up).astype(jnp.bfloat16)
    grad_gate_pre = (part_act * part_up * silu_slope).astype(jnp.bfloat16)
    grad_up_pre = (part_act * silu_val).astype(jnp.bfloat16)
    return (activated, grad_gate_pre, grad_up_pre)


def expert_terms(rows_in, rows_grad, weight_gate, weight_up, weight_down):
    part_gate = jnp.dot(rows_in, weight_gate, preferred_element_type=jnp.float32)
    part_up = jnp.dot(rows_in, weight_up, preferred_element_type=jnp.float32)
    part_act = contract_cols(rows_grad, weight_down)
    pre_gate, pre_up, grad_act = lax.psum((part_gate, part_up, part_act), "dp")
    activated, grad_gate_pre, grad_up_pre = hidden_products(pre_gate, pre_up, grad_act)
    back = contract_cols(grad_gate_pre, weight_gate) + contract_cols(grad_up_pre, weight_up)
    return (
        contract_rows(rows_in, grad_gate_pre),
        contract_rows(rows_in, grad_up_pre),
        contract_rows(activated, rows_grad),
        back,
    )


def shards(
    tokens,
    grad_out,
    route_ids,
    route_gates,
    w_gate,
    w_up,
    w_down,
    shared_gate,
    shared_up,
    shared_down,
):
    n_exp = lax.axis_size("expert")
    capacity = CAP
    grad_scale = 1.0 / n_exp
    targets = jnp.arange(n_exp, dtype=jnp.int32)
    matches = route_ids[:, :, None] == targets[None, None, :]
    chosen = jnp.any(matches, axis=1).astype(jnp.int32)
    gate_total = jnp.sum(jnp.where(matches, route_gates[:, :, None], 0.0), axis=1)
    slot_rank = jnp.cumsum(chosen, axis=0) - 1
    slot_ids = jnp.arange(capacity, dtype=jnp.int32)
    placement = (chosen[:, :, None] == 1) & (slot_rank[:, :, None] == slot_ids[None, None, :])
    place_bf = placement.astype(jnp.bfloat16)
    send_in = jnp.einsum(
        "tec,td->ecd", place_bf, tokens, preferred_element_type=jnp.float32
    ).astype(jnp.bfloat16)
    slot_gate = jnp.einsum("tec,te->ec", placement.astype(jnp.float32), gate_total)
    picked_grad = jnp.einsum("tec,td->ecd", place_bf, grad_out, preferred_element_type=jnp.float32)
    send_grad = (slot_gate[:, :, None] * picked_grad).astype(jnp.bfloat16)
    recv_in = lax.all_to_all(send_in, "expert", split_axis=0, concat_axis=0, tiled=True)
    recv_grad = lax.all_to_all(send_grad, "expert", split_axis=0, concat_axis=0, tiled=True)
    width_dev = tokens.shape[1]
    rows_in = recv_in.reshape(n_exp * capacity, width_dev)
    rows_grad = recv_grad.reshape(n_exp * capacity, width_dev)
    part_gate, part_up, part_down, back = expert_terms(
        rows_in, rows_grad, w_gate[0], w_up[0], w_down[0]
    )
    grad_gate = (part_gate * grad_scale).astype(jnp.bfloat16)[None]
    grad_up = (part_up * grad_scale).astype(jnp.bfloat16)[None]
    grad_down = (part_down * grad_scale).astype(jnp.bfloat16)[None]
    back_rows = lax.all_to_all(
        back.astype(jnp.bfloat16).reshape(n_exp, capacity, width_dev),
        "expert",
        split_axis=0,
        concat_axis=0,
        tiled=True,
    )
    routed = jnp.einsum("tec,ecd->td", place_bf, back_rows, preferred_element_type=jnp.float32)
    whole_gate, whole_up, whole_down = (
        lax.all_gather(shared_gate, "expert", axis=1, tiled=True),
        lax.all_gather(shared_up, "expert", axis=1, tiled=True),
        lax.all_gather(shared_down, "expert", axis=0, tiled=True),
    )
    own_gate, own_up, own_down, shared_back = expert_terms(
        tokens, grad_out, whole_gate, whole_up, whole_down
    )
    sum_gate, sum_up, sum_down = (
        lax.psum_scatter(own_gate, "expert", scatter_dimension=1, tiled=True),
        lax.psum_scatter(own_up, "expert", scatter_dimension=1, tiled=True),
        lax.psum_scatter(own_down, "expert", scatter_dimension=0, tiled=True),
    )
    grad_tokens = (shared_back + routed).astype(jnp.bfloat16)
    return (
        grad_tokens,
        grad_gate,
        grad_up,
        grad_down,
        sum_gate * grad_scale,
        sum_up * grad_scale,
        sum_down * grad_scale,
    )


def solution(mesh):
    in_specs = (
        P("expert", "dp"),
        P("expert", "dp"),
        P("expert", None),
        P("expert", None),
        P("expert", "dp", None),
        P("expert", "dp", None),
        P("expert", None, "dp"),
        P("dp", "expert"),
        P("dp", "expert"),
        P("expert", "dp"),
    )
    out_specs = (
        P("expert", "dp"),
        P("expert", "dp", None),
        P("expert", "dp", None),
        P("expert", None, "dp"),
        P("dp", "expert"),
        P("dp", "expert"),
        P("expert", "dp"),
    )
    return jax.shard_map(shards, mesh=mesh, in_specs=in_specs, out_specs=out_specs, check_vma=False)
```

profile of v0, /device:TPU:2, one launch (start us, length us, event | category | flops | bytes accessed | tf_op | source)
XLA Modules:
  0.0 1041.5 jit_solution(9965556063452526038)
XLA Ops:
  7.2 0.7 all-gather.4.cloned.1.call-update
  8.0 0.7 all-gather.6.cloned.1.call-update
  8.7 0.7 fusion.32
  9.4 0.6 reduce-window.6
  10.3 0.8 select_reduce_fusion
  11.5 1.4 fusion.17
  12.9 1.1 copy.36
  14.0 11.5 %all-to-all-start = ((bf16[32,12,896]{2,1,0:T(8,128)(2,1)}), bf16[32,12,896]{2,1,0:T(8,128)(2,1)S(1)}, u32[]{:S(2)}, u32[]{:S(2)}) async-start(bf16[32,12,896]{2,1,0:T(8,128)(2,1)} %copy.36), calls=%async_computation | async-start | bytes 1835008 | tf_op jit(solution)/shard_map/all_to_all | solution.py:79
  25.6 0.7 all-gather.8.cloned.1.call-update
  26.7 1.1 copy.37
  27.8 25.1 %all-to-all-done = bf16[32,12,896]{2,1,0:T(8,128)(2,1)S(1)} async-done(((bf16[32,12,896]{2,1,0:T(8,128)(2,1)}), bf16[32,12,896]{2,1,0:T(8,128)(2,1)S(1)}, u32[]{:S(2)}, u32[]{:S(2)}) %all-to-all-start) | async-done | bytes 688160 | tf_op jit(solution)/shard_map/all_to_all | solution.py:79
  53.0 4.9 all-to-all-start.1
  57.9 1.0 reshape.47
  58.9 28.4 %all-to-all-done.1 = bf16[32,12,896]{2,1,0:T(8,128)(2,1)} async-done(((bf16[32,12,896]{2,1,0:T(8,128)(2,1)}), bf16[32,12,896]{2,1,0:T(8,128)(2,1)}, u32[]{:S(2)}, u32[]{:S(2)}) %all-to-all-start.1) | async-done | bytes 688160 | tf_op jit(solution)/shard_map/all_to_all | solution.py:78
  87.3 1.3 reshape.48
  88.7 2.1 fusion.2
  90.8 2.1 fusion.6
  92.9 2.1 fusion.8
  95.1 1.8 all-gather.4.cloned.1.call-done
  96.9 3.2 fusion.40
  100.1 75.1 %all-gather.6.cloned.1.call-done = bf16[896,1024]{0,1:T(8,128)(2,1)} async-done(((bf16[896,32]{0,1:T(8,128)(2,1)}), bf16[896,1024]{0,1:T(8,128)(2,1)}) %all-gather.6.cloned.1.call-update) | async-done | bytes 1835024 | tf_op jit(solution)/shard_map/all_gather | solution.py:99
  175.2 3.2 fusion.41
  178.4 74.4 %all-gather.8.cloned.1.call-done = bf16[896,1024]{0,1:T(8,128)(2,1)} async-done(((bf16[896,32]{0,1:T(8,128)(2,1)}), bf16[896,1024]{0,1:T(8,128)(2,1)}) %all-gather.8.cloned.1.call-update) | async-done | bytes 1835024 | tf_op jit(solution)/shard_map/all_gather | solution.py:98
  252.8 3.2 fusion.42
  256.1 100.3 %all-reduce.3.cloned.1.call-done = (f32[384,1024]{1,0:T(8,128)}, f32[384,1024]{1,0:T(8,128)}, f32[384,1024]{1,0:T(8,128)}, f32[256,1024]{1,0:T(8,128)}, f32[256,1024]{1,0:T(8,128)}, /*index=5*/f32[256,1024]{1,0:T(8,128)}) async-done(((f32[384,1024]{1,0:T(8,128)}, f32[384,1024]{1,0:T(8,128)}, f32[384,1024]{1,0:T(8,128)}, f32[256,1024]{1,0:T(8,128)}, f32[256,1024]{1,0:T(8,128)}, ...) | async-done | bytes 7864336 | tf_op jit(solution)/shard_map/psum | solution.py:38
  356.4 4.1 fusion.25
  360.6 2.5 multiply_convert_fusion.7
  363.1 2.7 convolution_bitcast_fusion
  366.0 2.6 convolution_bitcast_fusion.1
  368.7 3.3 multiply_convert_fusion.4
  372.0 1.0 fusion
  373.1 0.9 copy-done.17
  374.1 1.9 fusion.18
  375.9 2.1 reshape.49
  378.0 10.2 all-to-all-start.2
  388.3 3.8 fusion.12
  392.1 2.4 fusion.11
  394.5 1.6 fusion.43
  396.7 2.5 fusion.13
  399.3 18.7 %all-to-all-done.2 = bf16[32,12,896]{2,1,0:T(8,128)(2,1)} async-done(((bf16[32,12,896]{2,1,0:T(8,128)(2,1)}), bf16[32,12,896]{2,1,0:T(8,128)(2,1)}, u32[]{:S(2)}, u32[]{:S(2)}) %all-to-all-start.2) | async-done | bytes 688160 | tf_op jit(solution)/shard_map/all_to_all | solution.py:89
  417.9 1.8 convolution_bitcast_fusion.2
  420.0 1.5 fusion.22
  421.5 167.4 %reduce-scatter.8.cloned.1.call-done = f32[32,896]{1,0:T(8,128)} async-done(((f32[1024,896]{1,0:T(8,128)}), f32[32,896]{1,0:T(8,128)}) %reduce-scatter.8.cloned.1.call-update) | async-done | bytes 114704 | tf_op jit(solution)/shard_map/reduce_scatter | solution.py:108
  588.8 1.6 broadcast_multiply_fusion
  590.4 220.8 %reduce-scatter.6.cloned.1.call-done = f32[896,32]{0,1:T(8,128)} async-done(((f32[896,1024]{0,1:T(8,128)}), f32[896,32]{0,1:T(8,128)}) %reduce-scatter.6.cloned.1.call-update) | async-done | bytes 114704 | tf_op jit(solution)/shard_map/reduce_scatter | solution.py:107
  811.2 1.6 broadcast_multiply_fusion.1
  812.8 220.3 %reduce-scatter.4.cloned.1.call-done = f32[896,32]{0,1:T(8,128)} async-done(((f32[896,1024]{0,1:T(8,128)}), f32[896,32]{0,1:T(8,128)}) %reduce-scatter.4.cloned.1.call-update) | async-done | bytes 114704 | tf_op jit(solution)/shard_map/reduce_scatter | solution.py:106
  1033.1 1.6 broadcast_multiply_fusion.2
  (56 shorter events, 2.5 us)
Async XLA Ops:
  7.2 81.5 %copy-start = (bf16[1,896,1024]{2,1,0:T(8,128)(2,1)S(1)}, bf16[1,896,1024]{2,1,0:T(8,128)(2,1)}, u32[]{:S(2)}) copy-start(bf16[1,896,1024]{2,1,0:T(8,128)(2,1)} %param.14) | copy-start | bytes 5505028
  7.2 89.7 %all-gather.4.cloned.1.call-start = ((), (), s32[]{:S(2)}) async-start(), calls=%async_computation.6 | async-start | bytes 1892352 | tf_op jit(solution)/shard_map/all_gather | solution.py:100
  7.9 167.2 %all-gather.6.cloned.1.call-start = ((), (), s32[]{:S(2)}) async-start(), calls=%async_computation.7 | async-start | bytes 1892352 | tf_op jit(solution)/shard_map/all_gather | solution.py:99
  12.9 13.4 %copy-start.1 = (bf16[256,896]{1,0:T(8,128)(2,1)S(1)}, bf16[256,896]{1,0:T(8,128)(2,1)}, u32[]{:S(2)}) copy-start(bf16[256,896]{1,0:T(8,128)(2,1)} %param.10) | copy-start | bytes 1376260
  14.0 38.9 %all-to-all-start = ((bf16[32,12,896]{2,1,0:T(8,128)(2,1)}), bf16[32,12,896]{2,1,0:T(8,128)(2,1)S(1)}, u32[]{:S(2)}, u32[]{:S(2)}) async-start(bf16[32,12,896]{2,1,0:T(8,128)(2,1)} %copy.36), calls=%async_computation | async-start | bytes 1835008 | tf_op jit(solution)/shard_map/all_to_all | solution.py:79
  25.5 227.2 %all-gather.8.cloned.1.call-start = ((), (), s32[]{:S(2)}) async-start(), calls=%async_computation.8 | async-start | bytes 1892352 | tf_op jit(solution)/shard_map/all_gather | solution.py:98
  53.0 34.4 %all-to-all-start.1 = ((bf16[32,12,896]{2,1,0:T(8,128)(2,1)}), bf16[32,12,896]{2,1,0:T(8,128)(2,1)}, u32[]{:S(2)}, u32[]{:S(2)}) async-start(bf16[32,12,896]{2,1,0:T(8,128)(2,1)} %copy.37), calls=%async_computation.1 | async-start | bytes 1835008 | tf_op jit(solution)/shard_map/all_to_all | solution.py:78
  57.9 298.6 %all-reduce.3.cloned.1.call-start = ((), (), s32[]{:S(2)}) async-start(), calls=%async_computation.12 | async-start | bytes 15728640 | tf_op jit(solution)/shard_map/psum | solution.py:38
  88.7 2.1 copy-start.13
  88.7 2.1 copy-start.16
  90.8 2.1 copy-start.11
  90.8 2.1 copy-start.15
  92.9 3.9 copy-start.5
  256.0 332.8 %reduce-scatter.8.cloned.1.call-start = ((), (), s32[]{:S(2)}) async-start(), calls=%async_computation.11 | async-start | bytes 3784704 | tf_op jit(solution)/shard_map/reduce_scatter | solution.py:108
  360.6 450.7 %reduce-scatter.6.cloned.1.call-start = ((), (), s32[]{:S(2)}) async-start(), calls=%async_computation.10 | async-start | bytes 3784704 | tf_op jit(solution)/shard_map/reduce_scatter | solution.py:107
  365.8 667.3 %reduce-scatter.4.cloned.1.call-start = ((), (), s32[]{:S(2)}) async-start(), calls=%async_computation.9 | async-start | bytes 3784704 | tf_op jit(solution)/shard_map/reduce_scatter | solution.py:106
  372.0 1.1 copy-start.8
  372.0 1.1 copy-start.10
  372.0 2.1 copy-start.17
  378.0 39.9 %all-to-all-start.2 = ((bf16[32,12,896]{2,1,0:T(8,128)(2,1)}), bf16[32,12,896]{2,1,0:T(8,128)(2,1)}, u32[]{:S(2)}, u32[]{:S(2)}) async-start(bf16[32,12,896]{2,1,0:T(8,128)(2,1)} %reshape.49), calls=%async_computation.2 | async-start | bytes 1835008 | tf_op jit(solution)/shard_map/all_to_all | solution.py:89
  388.2 3.9 copy-start.9
  388.2 3.9 copy-start.14
  392.1 2.4 copy-start.3
  392.1 4.0 copy-start.12
  394.5 1.7 copy-start.6
  394.5 2.2 copy-start.7
  417.9 1.8 copy-start.2
  417.9 2.0 copy-start.4
Sparse Core Ops, SparseCore 0:
  10.6 86.2 all-gather.3
  99.4 75.6 all-gather.5
  177.7 74.9 all-gather.7
  256.1 100.2 all-reduce.2
  360.7 228.1 reduce-scatter.7
  593.1 218.0 reduce-scatter.5
  815.1 217.9 reduce-scatter.3
where the time goes:
time: 1040 us
  waiting for transfers between devices  934 us (90%)
  matrix products  44 us (4%)
  starting transfers between devices  27.1 us (3%)
  between operations  14.4 us (1%)
  other arithmetic  12.7 us (1%)
    reduce_scatter x1, waiting for transfers between devices, shards(): lax.psum_scatter(own_up, 'expert', scatter_dimension=1, tiled=True)  221 us
    reduce_scatter x1, waiting for transfers between devices, shards(): lax.psum_scatter(own_gate, 'expert', scatter_dimension=1, tiled=True)  220 us
    reduce_scatter x1, waiting for transfers between devices, shards(): lax.psum_scatter(own_down, 'expert', scatter_dimension=0, tiled=True)  167 us
    psum x1, waiting for transfers between devices, expert_terms(): pre_gate, pre_up, grad_act = lax.psum((part_gate, part_up, part_act), 'dp')  100 us
    all_gather x1, waiting for transfers between devices, shards(): lax.all_gather(shared_up, 'expert', axis=1, tiled=True)  75.1 us
    all_gather x1, waiting for transfers between devices, shards(): lax.all_gather(shared_gate, 'expert', axis=1, tiled=True)  74.4 us
    all_to_all x1, waiting for transfers between devices, shards(): lax.all_to_all(send_in, 'expert', split_axis=0, concat_axis=0, tiled=True)  28.4 us
    all_to_all x1, waiting for transfers between devices, shards(): lax.all_to_all(send_grad, 'expert', split_axis=0, concat_axis=0, tiled=True)  25.1 us
  transfers between devices with their start and end apart: 10, of which 10 were waited for; matrix products, arithmetic and copies ran while one was open for 5% of the time, Pallas kernels for 0%

commit v1 on v0

--- a/solution.py
+++ b/solution.py
@@ -96,7 +96,9 @@
     routed = jnp.einsum("tec,ecd->td", place_bf, back_rows, preferred_element_type=jnp.float32)
     whole_gate, whole_up, whole_down = (
         lax.all_gather(shared_gate, "expert", axis=1, tiled=True),
-        lax.all_gather(shared_up, "expert", axis=1, tiled=True),
+        jnp.concatenate(
+            lax.all_to_all(jnp.stack([shared_up] * lax.axis_size("expert")), "expert", 0, 0), axis=1
+        ),
         lax.all_gather(shared_down, "expert", axis=0, tiled=True),
     )
     own_gate, own_up, own_down, shared_back = expert_terms(

time: 1040 us -> 967 us (0.930)
  waiting for transfers between devices: 934 us -> 822 us
  blocking collectives: 0 us -> 34.6 us
    all_gather x1 -> x0, waiting for transfers between devices: 75.1 us -> none  [shards(): lax.all_gather(shared_up, 'expert', axis=1, tiled=True)]
    all_gather x1, waiting for transfers between devices: 74.4 us -> 33.8 us  [shards(): lax.all_gather(shared_gate, 'expert', axis=1, tiled=True)]
    all_to_all x0 -> x1, blocking collectives: none -> 34.6 us  [shards(): lax.all_to_all(send_in, 'expert', split_axis=0, concat_axis=0, tiled=True)]
  transfers between devices with their start and end apart: 10 -> 9, of which waited for: 10 -> 8; matrix products, arithmetic and copies ran while one was open for 5% -> 6% of each run, Pallas kernels for 0% -> 0%
where the time goes in v1:
time: 967 us; the launch traced here: 966 us
  waiting for transfers between devices  822 us (85%)
  matrix products  45.5 us (5%)
  blocking collectives  34.6 us (4%)
  starting transfers between devices  27.3 us (3%)
  between operations  14.4 us (1%)
  other arithmetic  12.8 us (1%)
  local copies, waits for them, and re-layouts  9.91 us (1%)
    reduce_scatter x1, waiting for transfers between devices, shards(): lax.psum_scatter(own_up, 'expert', scatter_dimension=1, tiled=True)  221 us
    reduce_scatter x1, waiting for transfers between devices, shards(): lax.psum_scatter(own_gate, 'expert', scatter_dimension=1, tiled=True)  220 us
    reduce_scatter x1, waiting for transfers between devices, shards(): lax.psum_scatter(own_down, 'expert', scatter_dimension=0, tiled=True)  166 us
    psum x1, waiting for transfers between devices, expert_terms(): pre_gate, pre_up, grad_act = lax.psum((part_gate, part_up, part_act), 'dp')  100 us
    all_to_all x1, waiting for transfers between devices, shards(): lax.all_to_all(jnp.stack([shared_up] * lax.axis_size('expert')), 'expert'...  35 us
    all_to_all x1, blocking collectives, shards(): lax.all_to_all(send_in, 'expert', split_axis=0, concat_axis=0, tiled=True)  34.6 us
    all_gather x1, waiting for transfers between devices, shards(): lax.all_gather(shared_gate, 'expert', axis=1, tiled=True)  33.8 us
    all_to_all x1, waiting for transfers between devices, shards(): lax.all_to_all(send_grad, 'expert', split_axis=0, concat_axis=0, tiled=True)  25.8 us
  transfers between devices with their start and end apart: 9, of which 8 were waited for; matrix products, arithmetic and copies ran while one was open for 6% of the time, Pallas kernels for 0%

profile of v1, /device:TPU:2, one launch (start us, length us, event | category | flops | bytes accessed | tf_op | source)
XLA Modules:
  0.0 966.3 jit_solution(11065181936548942574)
XLA Ops:
  7.2 0.7 all-gather.3.cloned.1.call-update
  7.9 0.7 fusion.32
  8.7 0.7 select_reduce_fusion
  9.4 0.6 reduce-window.6
  10.7 1.4 fusion.17
  12.2 1.1 copy.37
  13.3 11.5 %all-to-all-start.1 = ((bf16[32,12,896]{2,1,0:T(8,128)(2,1)}), bf16[32,12,896]{2,1,0:T(8,128)(2,1)S(1)}, u32[]{:S(2)}, u32[]{:S(2)}) async-start(bf16[32,12,896]{2,1,0:T(8,128)(2,1)} %copy.37), calls=%async_computation.1 | async-start | bytes 1835008 | tf_op jit(solution)/shard_map/all_to_all | solution.py:79
  25.2 1.1 copy.38
  26.3 25.8 %all-to-all-done.1 = bf16[32,12,896]{2,1,0:T(8,128)(2,1)S(1)} async-done(((bf16[32,12,896]{2,1,0:T(8,128)(2,1)}), bf16[32,12,896]{2,1,0:T(8,128)(2,1)S(1)}, u32[]{:S(2)}, u32[]{:S(2)}) %all-to-all-start.1) | async-done | bytes 688160 | tf_op jit(solution)/shard_map/all_to_all | solution.py:79
  52.2 34.6 %all_to_all.20 = bf16[32,12,896]{2,1,0:T(8,128)(2,1)} all-to-all(bf16[32,12,896]{2,1,0:T(8,128)(2,1)} %copy.38), channel_id=1, replica_groups=mesh['dp'=8,'expert'=32] {'expert'}, dimensions={0} | all-to-all | bytes 1376256 | tf_op jit(solution)/shard_map/all_to_all | solution.py:78
  86.7 1.4 stack.2
  88.1 5.2 all-to-all-start
  93.3 0.7 all-gather.5.cloned.1.call-update
  94.1 1.0 reshape.57
  95.1 1.3 reshape.58
  96.4 2.1 fusion.2
  98.6 2.1 fusion.6
  100.7 2.2 fusion.8
  102.8 35.0 %all-to-all-done = bf16[32,896,32]{1,2,0:T(8,128)(2,1)} async-done(((bf16[32,896,32]{1,2,0:T(8,128)(2,1)}), bf16[32,896,32]{1,2,0:T(8,128)(2,1)}, u32[]{:S(2)}, u32[]{:S(2)}) %all-to-all-start) | async-done | bytes 1835040 | tf_op jit(solution)/shard_map/all_to_all | solution.py:100
  137.8 3.3 fusion.41
  141.1 3.2 fusion.40
  144.3 33.8 %all-gather.5.cloned.1.call-done = bf16[896,1024]{0,1:T(8,128)(2,1)} async-done(((bf16[896,32]{0,1:T(8,128)(2,1)}), bf16[896,1024]{0,1:T(8,128)(2,1)}) %all-gather.5.cloned.1.call-update) | async-done | bytes 1835024 | tf_op jit(solution)/shard_map/all_gather | solution.py:98
  178.1 3.2 fusion.42
  181.4 100.4 %all-reduce.3.cloned.1.call-done = (f32[384,1024]{1,0:T(8,128)}, f32[384,1024]{1,0:T(8,128)}, f32[384,1024]{1,0:T(8,128)}, f32[256,1024]{1,0:T(8,128)}, f32[256,1024]{1,0:T(8,128)}, /*index=5*/f32[256,1024]{1,0:T(8,128)}) async-done(((f32[384,1024]{1,0:T(8,128)}, f32[384,1024]{1,0:T(8,128)}, f32[384,1024]{1,0:T(8,128)}, f32[256,1024]{1,0:T(8,128)}, f32[256,1024]{1,0:T(8,128)}, ...) | async-done | bytes 7864336 | tf_op jit(solution)/shard_map/psum | solution.py:38
  281.7 4.1 fusion.25
  285.9 2.5 multiply_convert_fusion.7
  288.4 2.7 convolution_bitcast_fusion
  291.3 2.6 convolution_bitcast_fusion.1
  294.0 3.3 multiply_convert_fusion.4
  297.3 1.0 fusion
  298.4 0.9 copy-done.17
  299.4 1.9 fusion.18
  301.2 2.1 reshape.59
  303.3 10.2 %all-to-all-start.3 = ((bf16[32,12,896]{2,1,0:T(8,128)(2,1)}), bf16[32,12,896]{2,1,0:T(8,128)(2,1)}, u32[]{:S(2)}, u32[]{:S(2)}) async-start(bf16[32,12,896]{2,1,0:T(8,128)(2,1)} %reshape.59), calls=%async_computation.3 | async-start | bytes 1835008 | tf_op jit(solution)/shard_map/all_to_all | solution.py:89
  313.6 3.8 fusion.12
  317.4 2.4 fusion.11
  319.8 1.7 fusion.43
  321.5 0.5 copy-done.6
  322.0 2.5 fusion.13
  324.6 18.7 %all-to-all-done.3 = bf16[32,12,896]{2,1,0:T(8,128)(2,1)} async-done(((bf16[32,12,896]{2,1,0:T(8,128)(2,1)}), bf16[32,12,896]{2,1,0:T(8,128)(2,1)}, u32[]{:S(2)}, u32[]{:S(2)}) %all-to-all-start.3) | async-done | bytes 688160 | tf_op jit(solution)/shard_map/all_to_all | solution.py:89
  343.3 1.7 convolution_bitcast_fusion.2
  345.0 3.0 fusion.22
  348.0 166.1 %reduce-scatter.8.cloned.1.call-done = f32[32,896]{1,0:T(8,128)} async-done(((f32[1024,896]{1,0:T(8,128)}), f32[32,896]{1,0:T(8,128)}) %reduce-scatter.8.cloned.1.call-update) | async-done | bytes 114704 | tf_op jit(solution)/shard_map/reduce_scatter | solution.py:110
  514.0 1.6 broadcast_multiply_fusion
  515.6 220.6 %reduce-scatter.6.cloned.1.call-done = f32[896,32]{0,1:T(8,128)} async-done(((f32[896,1024]{0,1:T(8,128)}), f32[896,32]{0,1:T(8,128)}) %reduce-scatter.6.cloned.1.call-update) | async-done | bytes 114704 | tf_op jit(solution)/shard_map/reduce_scatter | solution.py:109
  736.2 1.6 broadcast_multiply_fusion.1
  737.8 220.1 %reduce-scatter.4.cloned.1.call-done = f32[896,32]{0,1:T(8,128)} async-done(((f32[896,1024]{0,1:T(8,128)}), f32[896,32]{0,1:T(8,128)}) %reduce-scatter.4.cloned.1.call-update) | async-done | bytes 114704 | tf_op jit(solution)/shard_map/reduce_scatter | solution.py:108
  957.9 1.6 broadcast_multiply_fusion.2
  (55 shorter events, 1.7 us)
Async XLA Ops:
  7.2 89.2 %copy-start = (bf16[1,896,1024]{2,1,0:T(8,128)(2,1)S(1)}, bf16[1,896,1024]{2,1,0:T(8,128)(2,1)}, u32[]{:S(2)}) copy-start(bf16[1,896,1024]{2,1,0:T(8,128)(2,1)} %param.14) | copy-start | bytes 5505028
  7.2 133.9 %all-gather.3.cloned.1.call-start = ((), (), s32[]{:S(2)}) async-start(), calls=%async_computation.7 | async-start | bytes 1892352 | tf_op jit(solution)/shard_map/all_gather | solution.py:102
  12.1 12.7 %copy-start.1 = (bf16[256,896]{1,0:T(8,128)(2,1)S(1)}, bf16[256,896]{1,0:T(8,128)(2,1)}, u32[]{:S(2)}) copy-start(bf16[256,896]{1,0:T(8,128)(2,1)} %param.10) | copy-start | bytes 1376260
  13.3 38.9 %all-to-all-start.1 = ((bf16[32,12,896]{2,1,0:T(8,128)(2,1)}), bf16[32,12,896]{2,1,0:T(8,128)(2,1)S(1)}, u32[]{:S(2)}, u32[]{:S(2)}) async-start(bf16[32,12,896]{2,1,0:T(8,128)(2,1)} %copy.37), calls=%async_computation.1 | async-start | bytes 1835008 | tf_op jit(solution)/shard_map/all_to_all | solution.py:79
  25.2 61.5 %copy-start.14 = (bf16[896,32]{0,1:T(8,128)(2,1)S(1)}, bf16[896,32]{0,1:T(8,128)(2,1)}, u32[]{:S(2)}) copy-start(bf16[896,32]{0,1:T(8,128)(2,1)} %param.18) | copy-start | bytes 172036
  88.1 49.7 %all-to-all-start = ((bf16[32,896,32]{1,2,0:T(8,128)(2,1)}), bf16[32,896,32]{1,2,0:T(8,128)(2,1)}, u32[]{:S(2)}, u32[]{:S(2)}) async-start(bf16[32,896,32]{1,2,0:T(8,128)(2,1)} %stack.2), calls=%async_computation | async-start | bytes 3670016 | tf_op jit(solution)/shard_map/all_to_all | solution.py:100
  93.3 84.8 %all-gather.5.cloned.1.call-start = ((), (), s32[]{:S(2)}) async-start(), calls=%async_computation.8 | async-start | bytes 1892352 | tf_op jit(solution)/shard_map/all_gather | solution.py:98
  94.0 187.7 %all-reduce.3.cloned.1.call-start = ((), (), s32[]{:S(2)}) async-start(), calls=%async_computation.12 | async-start | bytes 15728640 | tf_op jit(solution)/shard_map/psum | solution.py:38
  96.4 2.1 copy-start.12
  96.4 2.1 copy-start.16
  98.6 2.1 copy-start.10
  98.6 2.1 copy-start.15
  102.8 38.3 %copy-start.4 = (bf16[256,896]{1,0:T(8,128)(2,1)S(1)}, bf16[256,896]{1,0:T(8,128)(2,1)}, u32[]{:S(2)}) copy-start(bf16[256,896]{1,0:T(8,128)(2,1)} %param.11) | copy-start | bytes 1376260
  181.3 332.7 %reduce-scatter.8.cloned.1.call-start = ((), (), s32[]{:S(2)}) async-start(), calls=%async_computation.11 | async-start | bytes 3784704 | tf_op jit(solution)/shard_map/reduce_scatter | solution.py:110
  285.9 450.3 %reduce-scatter.6.cloned.1.call-start = ((), (), s32[]{:S(2)}) async-start(), calls=%async_computation.10 | async-start | bytes 3784704 | tf_op jit(solution)/shard_map/reduce_scatter | solution.py:109
  291.1 666.7 %reduce-scatter.4.cloned.1.call-start = ((), (), s32[]{:S(2)}) async-start(), calls=%async_computation.9 | async-start | bytes 3784704 | tf_op jit(solution)/shard_map/reduce_scatter | solution.py:108
  297.3 1.1 copy-start.7
  297.3 1.1 copy-start.9
  297.3 2.1 copy-start.17
  303.3 39.9 %all-to-all-start.3 = ((bf16[32,12,896]{2,1,0:T(8,128)(2,1)}), bf16[32,12,896]{2,1,0:T(8,128)(2,1)}, u32[]{:S(2)}, u32[]{:S(2)}) async-start(bf16[32,12,896]{2,1,0:T(8,128)(2,1)} %reshape.59), calls=%async_computation.3 | async-start | bytes 1835008 | tf_op jit(solution)/shard_map/all_to_all | solution.py:89
  313.5 3.9 copy-start.8
  313.5 3.9 copy-start.13
  317.4 2.4 copy-start.2
  317.4 4.1 copy-start.11
  319.8 1.7 copy-start.5
  319.8 2.2 copy-start.6
  343.2 1.7 copy-start.3
Sparse Core Ops, SparseCore 0:
  10.6 85.5 all-gather.2
  98.8 79.2 all-gather.4
  181.5 100.2 all-reduce.2
  286.0 228.0 reduce-scatter.7
  518.3 217.8 reduce-scatter.5
  739.9 217.8 reduce-scatter.3
